TPU v7x, 32 devices: a whole 2x2x4 slice. The times are simulated.
32 devices in a mesh: batch: 8 (over y, x, core), mp: 4 (over z).
Axes of the slice: x: 2, y: 2, z: 4, core: 2. Of those that a mesh axis runs over, the one named last changes fastest.
Arguments:
- token_ids: int32 [8, 1536], P('batch'), may hold values from 0 to 30527
- segment_ids: int32 [8, 1536], P('batch'), may hold values from 0 to 8, never falling along the last dimension, each value on 1 to 1024 neighbouring positions
- row_of: int32 [30528], replicated, may hold values from 0 to 30527, each once
- query_count: int32 [1], replicated, may hold values from 16 to 32
- table: float32 [30528, 768], P('batch'), may hold values from -8 to 8
- qkv_weight: float32 [768, 3, 768], P('batch', None, 'mp'), may hold values from -0.21875 to 0.21875
- out_weight: float32 [768, 768], P('mp', 'batch'), may hold values from -0.875 to 0.875
- gate_up_weight: float32 [768, 2, 3072], P('batch', None, 'mp'), may hold values from -0.21875 to 0.21875
- down_weight: float32 [3072, 768], P('mp', 'batch'), may hold values from -0.109375 to 0.109375
- gains: float32 [2, 768], P(None, 'batch'), may hold values from 0.3 to 2.5
- table_m: float32 [30528, 768], P('batch'), may hold values from -0.0009765625 to 0.0009765625
- qkv_m: float32 [768, 3, 768], P('batch', None, 'mp'), may hold values from -0.0009765625 to 0.0009765625
- out_m: float32 [768, 768], P('mp', 'batch'), may hold values from -0.0009765625 to 0.0009765625
- gate_up_m: float32 [768, 2, 3072], P('batch', None, 'mp'), may hold values from -0.0009765625 to 0.0009765625
- down_m: float32 [3072, 768], P('mp', 'batch'), may hold values from -0.0009765625 to 0.0009765625
- gains_m: float32 [2, 768], P(None, 'batch'), may hold values from -0.0009765625 to 0.0009765625
- table_v: float32 [30528, 768], P('batch'), may hold values from 3.040972e-08 to 1.2163888e-07
- qkv_v: float32 [768, 3, 768], P('batch', None, 'mp'), may hold values from 3.040972e-08 to 1.2163888e-07
- out_v: float32 [768, 768], P('mp', 'batch'), may hold values from 3.040972e-08 to 1.2163888e-07
- gate_up_v: float32 [768, 2, 3072], P('batch', None, 'mp'), may hold values from 3.040972e-08 to 1.2163888e-07
- down_v: float32 [3072, 768], P('mp', 'batch'), may hold values from 3.040972e-08 to 1.2163888e-07
- gains_v: float32 [2, 768], P(None, 'batch'), may hold values from 3.040972e-08 to 1.2163888e-07
Outputs:
- loss: float32 [1], replicated
- grad_norm: float32 [1], replicated
- new_table: float32 [30528, 768], P('batch')
- new_qkv_weight: float32 [768, 3, 768], P('batch', None, 'mp')
- new_out_weight: float32 [768, 768], P('mp', 'batch')
- new_gate_up_weight: float32 [768, 2, 3072], P('batch', None, 'mp')
- new_down_weight: float32 [3072, 768], P('mp', 'batch')
- new_gains: float32 [2, 768], P(None, 'batch')
- clipped_table_grad: float32 [30528, 768], P('batch')
- new_qkv_m: float32 [768, 3, 768], P('batch', None, 'mp')
- new_out_m: float32 [768, 768], P('mp', 'batch')
- new_gate_up_m: float32 [768, 2, 3072], P('batch', None, 'mp')
- new_down_m: float32 [3072, 768], P('mp', 'batch')
- new_gains_m: float32 [2, 768], P(None, 'batch')
- new_table_v: float32 [30528, 768], P('batch')
- new_qkv_v: float32 [768, 3, 768], P('batch', None, 'mp')
- new_out_v: float32 [768, 768], P('mp', 'batch')
- new_gate_up_v: float32 [768, 2, 3072], P('batch', None, 'mp')
- new_down_v: float32 [3072, 768], P('mp', 'batch')
- new_gains_v: float32 [2, 768], P(None, 'batch')
Inputs may be any that keep to these rules, and one draw needn't show every extreme that they name: `segment_ids`: in each row the ids never fall, every id 0 to 8 appears, id 8 marks padding, each segment has 1 to 1024 tokens and one has exactly 1024. A permutation: token t's embedding is table row row_of[t]. The first query_count queries count.
All inputs are finite; a program needn't handle non-finite values.
Results may differ from a plain program's by a relative error of at most 0.0075.
The roundings to bfloat16 on the way count: a program that leaves them out, or rounds other values in their place, can miss the bound.
Values may be sent and summed in bfloat16 or wider, within the bound.
A program may use at most 320 MiB of HBM per device.

v0:
```python
from functools import partial
import jax
import jax.numpy as jnp
from jax import lax
from jax.sharding import PartitionSpec as P

D = 768
HEAD_DIM = 64
SEGS = 8
peak_affinity = lax.Precision.HIGHEST
sharpness_divisor = 0.05
clip_limit = 1.0
step_number = 3.0
rates = (0.3, 0.02, 0.02, 0.02, 0.02, 0.3)
negative = -1e30


def positions(segment_row, segment_count):
    labels = jnp.arange(segment_count + 1, dtype=jnp.int32)
    member = (segment_row[:, None] == labels[None, :]).astype(jnp.int32)
    counts = jnp.sum(member, 0)
    starts = jnp.cumsum(counts) - counts
    first_index = jnp.sum(member * starts[None, :], 1)
    return (jnp.arange(segment_row.shape[0], dtype=jnp.int32) - first_index).astype(jnp.float32)


def rotate(values, places):
    half_dim = values.shape[-1] // 2
    freqs = jnp.power(1000.0, -2.0 * jnp.arange(half_dim, dtype=jnp.float32) / values.shape[-1])
    angles = places[:, None] * freqs[None, :]
    cosine = jnp.cos(angles)[:, None, :]
    sine = jnp.sin(angles)[:, None, :]
    former = values[..., :half_dim]
    latter = values[..., half_dim:]
    return jnp.concatenate([former * cosine - latter * sine, latter * cosine + former * sine], -1)


def layer_norm(values, gain):
    centred = values - jnp.mean(values, -1, keepdims=True)
    spread = jnp.mean(centred * centred, -1, keepdims=True)
    return centred * lax.rsqrt(spread + 1e-05) * gain


def swiglu(gate_up):
    return jax.nn.silu(gate_up[:, 0]) * gate_up[:, 1]


def contract(left, right, left_dim, right_dim):
    return lax.dot_general(
        left, right, (((left_dim,), (right_dim,)), ((), ())), preferred_element_type=jnp.float32
    )


def pool_rows(hidden, segment_ids):
    rows_dev, length = segment_ids.shape
    labels = jnp.arange(SEGS, dtype=jnp.int32)
    member = (segment_ids[:, None, :] == labels[None, :, None]).astype(jnp.float32)
    sums = jnp.einsum(
        "rsl,rld->rsd", member, hidden.reshape(rows_dev, length, -1), precision=peak_affinity
    )
    pooled = (sums / jnp.sum(member, -1, keepdims=True)).reshape(rows_dev * SEGS, -1)
    return pooled * lax.rsqrt(jnp.sum(pooled * pooled, -1, keepdims=True) + 1e-06)


def block_scores(query_block, key_row, segment_block, segment_row):
    scores = jnp.einsum(
        "qhd,khd->hqk", query_block, key_row, preferred_element_type=jnp.float32
    ) * HEAD_DIM ** (-0.5)
    same = segment_block[:, None] == segment_row[None, :]
    return jnp.where(same[None], scores, negative)


def attend(query, keys, values, segment_ids, width):
    rows_dev, length = segment_ids.shape
    per_row = length // width
    flat_segments = segment_ids.reshape(-1)

    def one_block(block):
        row_index = block // per_row
        query_block = lax.dynamic_slice_in_dim(query, block * width, width, 0)
        segment_block = lax.dynamic_slice_in_dim(flat_segments, block * width, width, 0)
        scores = block_scores(query_block, keys[row_index], segment_block, segment_ids[row_index])
        peak_score = jnp.max(scores, -1, keepdims=True)
        weights = jnp.exp(scores - peak_score)
        totals = jnp.sum(weights, -1, keepdims=True)
        probs = (weights / totals).astype(jnp.bfloat16)
        output = jnp.einsum(
            "hqk,khd->qhd", probs, values[row_index], preferred_element_type=jnp.float32
        )
        return (output, (peak_score + jnp.log(totals))[..., 0])

    outputs, log_totals = lax.map(one_block, jnp.arange(rows_dev * per_row, dtype=jnp.int32))
    return (outputs.reshape((rows_dev * length,) + outputs.shape[2:]), log_totals)


def attend_back(query, keys, values, segment_ids, log_totals, grad_out, width):
    rows_dev, length = segment_ids.shape
    per_row = length // width
    flat_segments = segment_ids.reshape(-1)
    factor = HEAD_DIM ** (-0.5)

    def one_block(carry, block):
        grad_keys, grad_values = carry
        row_index = block // per_row
        query_block = lax.dynamic_slice_in_dim(query, block * width, width, 0)
        segment_block = lax.dynamic_slice_in_dim(flat_segments, block * width, width, 0)
        grad_block = lax.dynamic_slice_in_dim(grad_out, block * width, width, 0)
        scores = block_scores(query_block, keys[row_index], segment_block, segment_ids[row_index])
        probs = jnp.exp(scores - log_totals[block][..., None])
        grad_probs = jnp.einsum(
            "qhd,khd->hqk", grad_block, values[row_index], preferred_element_type=jnp.float32
        )
        inner = jnp.sum(probs * grad_probs, -1, keepdims=True)
        grad_scores = (probs * (grad_probs - inner)).astype(jnp.bfloat16)
        grad_query = (
            jnp.einsum(
                "hqk,khd->qhd", grad_scores, keys[row_index], preferred_element_type=jnp.float32
            )
            * factor
        )
        key_term = (
            jnp.einsum("hqk,qhd->khd", grad_scores, query_block, preferred_element_type=jnp.float32)
            * factor
        )
        value_term = jnp.einsum(
            "hqk,qhd->khd",
            probs.astype(jnp.bfloat16),
            grad_block,
            preferred_element_type=jnp.float32,
        )
        return (
            (grad_keys.at[row_index].add(key_term), grad_values.at[row_index].add(value_term)),
            grad_query,
        )

    zeros = jnp.zeros(keys.shape, jnp.float32)
    (grad_keys, grad_values), grad_query = lax.scan(
        one_block, (zeros, zeros), jnp.arange(rows_dev * per_row, dtype=jnp.int32)
    )
    return (grad_query.reshape((rows_dev * length,) + grad_query.shape[2:]), grad_keys, grad_values)


def adam_update(weight, grad, first, second, rate):
    first = 0.5 * first + 0.5 * grad
    second = 0.5 * second + 0.5 * grad * grad
    correction = 1.0 - 0.5**step_number
    weight = weight - rate * (
        first / correction / (jnp.sqrt(second / correction) + 1e-08) + 0.01 * weight
    )
    return (weight, first, second)


def local(
    token_ids,
    segment_ids,
    row_of,
    query_count,
    table,
    qkv_weight,
    out_weight,
    gate_up_weight,
    down_weight,
    gains,
    table_m,
    qkv_m,
    out_m,
    gate_up_m,
    down_m,
    gains_m,
    table_v,
    qkv_v,
    out_v,
    gate_up_v,
    down_v,
    gains_v,
):
    local_width = table.shape[1] // lax.axis_size("mp")
    column = lax.axis_index("mp") * local_width
    table_cols = lax.dynamic_slice_in_dim(table, column, local_width, 1)
    low_table, w_qkv, w_out, w_gu, w_down, gain_low = (
        lax.all_gather(table_cols.astype(jnp.bfloat16), "batch", axis=0, tiled=True),
        lax.all_gather(qkv_weight.astype(jnp.bfloat16), "batch", axis=0, tiled=True),
        lax.all_gather(out_weight.astype(jnp.bfloat16), "batch", axis=1, tiled=True),
        lax.all_gather(gate_up_weight.astype(jnp.bfloat16), "batch", axis=0, tiled=True),
        lax.all_gather(down_weight.astype(jnp.bfloat16), "batch", axis=1, tiled=True),
        lax.all_gather(gains.astype(jnp.bfloat16), "batch", axis=1, tiled=True),
    )
    gain = gain_low.astype(jnp.float32)
    rows_dev, length = token_ids.shape
    tokens = rows_dev * length
    width = min(512, length)
    heads_local = w_qkv.shape[2] // HEAD_DIM
    ff_local = w_gu.shape[2]
    table_rows = row_of[token_ids.reshape(-1)]
    x_zero = lax.all_gather(low_table[table_rows], "mp", axis=1, tiled=True)
    places = jax.vmap(partial(positions, segment_count=SEGS))(segment_ids).reshape(-1)
    qkv = jnp.dot(x_zero, w_qkv.reshape(D, -1), preferred_element_type=jnp.float32).reshape(
        tokens, 3, heads_local, HEAD_DIM
    )
    query = rotate(qkv[:, 0], places).astype(jnp.bfloat16)
    keys = (
        rotate(qkv[:, 1], places)
        .astype(jnp.bfloat16)
        .reshape(rows_dev, length, heads_local, HEAD_DIM)
    )
    values = qkv[:, 2].astype(jnp.bfloat16).reshape(rows_dev, length, heads_local, HEAD_DIM)
    attended, log_totals = attend(query, keys, values, segment_ids, width)
    attended_low = attended.reshape(tokens, -1).astype(jnp.bfloat16)
    attn_term = jnp.dot(attended_low, w_out, preferred_element_type=jnp.float32)
    attn = lax.psum(attn_term, "mp")
    hidden_one, first_back = jax.vjp(layer_norm, x_zero.astype(jnp.float32) + attn, gain[0])
    hidden_low = hidden_one.astype(jnp.bfloat16)
    gate_up = jnp.dot(hidden_low, w_gu.reshape(D, -1), preferred_element_type=jnp.float32).reshape(
        tokens, 2, ff_local
    )
    active, swiglu_back = jax.vjp(swiglu, gate_up)
    active_low = active.astype(jnp.bfloat16)
    mlp = lax.psum(jnp.dot(active_low, w_down, preferred_element_type=jnp.float32), "mp")
    hidden_two, second_back = jax.vjp(layer_norm, hidden_one + mlp, gain[1])
    embed, pool_back = jax.vjp(lambda hidden: pool_rows(hidden, segment_ids), hidden_two)
    batch_index = lax.axis_index("batch")
    half_count = lax.axis_size("batch") // 2
    texts = embed.shape[0]
    queries_all = half_count * texts
    everyone = lax.all_gather(embed, "batch", axis=0, tiled=True)
    question_vectors = everyone[:queries_all]
    passage_vectors = everyone[queries_all:]
    limit = query_count[0].astype(jnp.float32)
    labels = jnp.arange(queries_all, dtype=jnp.int32)
    weight_rows = (labels < query_count[0]).astype(jnp.float32) / limit
    affinity_scores = (
        jnp.dot(question_vectors, passage_vectors.T, precision=peak_affinity) / sharpness_divisor
    )
    target = (labels[:, None] == labels[None, :]).astype(jnp.float32)
    loss_value = jnp.sum(
        weight_rows
        * (jax.nn.logsumexp(affinity_scores, -1) - jnp.sum(affinity_scores * target, -1))
    )
    affinity_derivative = (jax.nn.softmax(affinity_scores, -1) - target) * weight_rows[:, None]
    grad_all = jnp.concatenate(
        [
            jnp.dot(affinity_derivative, passage_vectors, precision=peak_affinity)
            / sharpness_divisor,
            jnp.dot(affinity_derivative.T, question_vectors, precision=peak_affinity)
            / sharpness_divisor,
        ],
        0,
    )
    grad_embed = lax.dynamic_slice_in_dim(grad_all, batch_index * texts, texts, 0)
    (grad_two,) = pool_back(grad_embed)
    grad_second, grad_gain_two = second_back(grad_two)
    grad_mlp_low = grad_second.astype(jnp.bfloat16)
    grad_active = contract(grad_mlp_low, w_down, 1, 1)
    grad_down = contract(active_low, grad_mlp_low, 0, 0)
    (grad_gate_up,) = swiglu_back(grad_active)
    grad_gu_low = grad_gate_up.reshape(tokens, -1).astype(jnp.bfloat16)
    back_term = contract(grad_gu_low, w_gu.reshape(D, -1), 1, 1)
    grad_one = grad_second + lax.psum(back_term, "mp")
    grad_first, grad_gain_one = first_back(grad_one)
    grad_gu = contract(hidden_low, grad_gu_low, 0, 0)
    grad_attn_low = grad_first.astype(jnp.bfloat16)
    grad_attended = contract(grad_attn_low, w_out, 1, 1).astype(jnp.bfloat16)
    grad_out = contract(attended_low, grad_attn_low, 0, 0)
    grad_query, grad_keys, grad_values = attend_back(
        query,
        keys,
        values,
        segment_ids,
        log_totals,
        grad_attended.reshape(tokens, heads_local, HEAD_DIM),
        width,
    )
    _, rotate_back = jax.vjp(lambda inputs: rotate(inputs, places), qkv[:, 0])
    (grad_query_raw,) = rotate_back(grad_query)
    (grad_key_raw,) = rotate_back(grad_keys.reshape(tokens, heads_local, HEAD_DIM))
    grad_qkv_low = (
        jnp.stack(
            [grad_query_raw, grad_key_raw, grad_values.reshape(tokens, heads_local, HEAD_DIM)], 1
        )
        .reshape(tokens, -1)
        .astype(jnp.bfloat16)
    )
    grad_zero = grad_first + lax.psum(contract(grad_qkv_low, w_qkv.reshape(D, -1), 1, 1), "mp")
    grad_qkv = contract(x_zero, grad_qkv_low, 0, 0)
    grad_table = (
        jnp.zeros((low_table.shape[0], local_width), jnp.float32)
        .at[table_rows]
        .add(lax.dynamic_slice_in_dim(grad_zero, column, local_width, 1))
    )
    grad_gains = jnp.stack([grad_gain_one, grad_gain_two], 0)
    reduced = (
        lax.psum_scatter(grad_table, "batch", scatter_dimension=0, tiled=True),
        lax.psum_scatter(grad_qkv.reshape(D, 3, -1), "batch", scatter_dimension=0, tiled=True),
        lax.psum_scatter(grad_out, "batch", scatter_dimension=1, tiled=True),
        lax.psum_scatter(grad_gu.reshape(D, 2, -1), "batch", scatter_dimension=0, tiled=True),
        lax.psum_scatter(grad_down, "batch", scatter_dimension=1, tiled=True),
        lax.psum_scatter(grad_gains, "batch", scatter_dimension=1, tiled=True),
    )
    squares = sum((jnp.sum(part * part) for part in reduced[:5])) + jnp.sum(
        reduced[5] * reduced[5]
    ) / lax.axis_size("mp")
    table_full = lax.all_gather(reduced[0], "mp", axis=1, tiled=True)
    total_squares = lax.psum(squares, ("batch", "mp"))
    grad_norm = jnp.sqrt(total_squares)
    scale = clip_limit / jnp.maximum(grad_norm, clip_limit)
    olds = (table, qkv_weight, out_weight, gate_up_weight, down_weight, gains)
    grads_all = (table_full,) + tuple(reduced[1:])
    firsts = (table_m, qkv_m, out_m, gate_up_m, down_m, gains_m)
    seconds = (table_v, qkv_v, out_v, gate_up_v, down_v, gains_v)
    updated = [
        adam_update(weight_old, grad_part * scale, first_old, second_old, rate)
        for weight_old, grad_part, first_old, second_old, rate in zip(
            olds, grads_all, firsts, seconds, rates
        )
    ]
    clipped_table = table_full * scale
    loss = loss_value.reshape(1)
    return (
        loss,
        grad_norm.reshape(1),
        updated[0][0],
        updated[1][0],
        updated[2][0],
        updated[3][0],
        updated[4][0],
        updated[5][0],
        clipped_table,
        updated[1][1],
        updated[2][1],
        updated[3][1],
        updated[4][1],
        updated[5][1],
        updated[0][2],
        updated[1][2],
        updated[2][2],
        updated[3][2],
        updated[4][2],
        updated[5][2],
    )


def solution(mesh):
    placed = (
        P("batch", None),
        P("batch", None),
        P(),
        P(),
        P("batch", None),
        P("batch", None, "mp"),
        P("mp", "batch"),
        P("batch", None, "mp"),
        P("mp", "batch"),
        P(None, "batch"),
        P("batch", None),
        P("batch", None, "mp"),
        P("mp", "batch"),
        P("batch", None, "mp"),
        P("mp", "batch"),
        P(None, "batch"),
        P("batch", None),
        P("batch", None, "mp"),
        P("mp", "batch"),
        P("batch", None, "mp"),
        P("mp", "batch"),
        P(None, "batch"),
    )
    return jax.shard_map(
        local,
        mesh=mesh,
        in_specs=placed,
        out_specs=(
            P(),
            P(),
            P("batch", None),
            P("batch", None, "mp"),
            P("mp", "batch"),
            P("batch", None, "mp"),
            P("mp", "batch"),
            P(None, "batch"),
            P("batch", None),
            P("batch", None, "mp"),
            P("mp", "batch"),
            P("batch", None, "mp"),
            P("mp", "batch"),
            P(None, "batch"),
            P("batch", None),
            P("batch", None, "mp"),
            P("mp", "batch"),
            P("batch", None, "mp"),
            P("mp", "batch"),
            P(None, "batch"),
        ),
        check_vma=False,
    )
```

profile of v0, /device:TPU:0, one launch (start us, length us, event | category | flops | bytes accessed | tf_op | source)
XLA Modules:
  0.0 1895.6 jit_solution(3074774490312549609)
XLA Ops:
  7.3 12.4 copy.141
  31.4 63.1 %all-gather.17.cloned.1.call-done = bf16[8,3816,192]{1,2,0:T(8,128)(2,1)} async-done(((bf16[1,3816,192]{1,2,0:T(8,128)(2,1)}), bf16[8,3816,192]{1,2,0:T(8,128)(2,1)}) %all-gather.17.cloned.1.call-update) | async-done | bytes 11722768 | tf_op jit(solution)/shard_map/all_gather | solution.py:181
  94.5 18.1 copy.142
  112.6 11.2 gather_fusion.1
  126.6 13.2 all_gather.29
  151.9 23.6 %all-gather.15.cloned.1.call-done = bf16[1536,768]{0,1:T(8,128)(2,1)} async-done(((bf16[1536,192]{0,1:T(8,128)(2,1)}), bf16[1536,768]{0,1:T(8,128)(2,1)}) %all-gather.15.cloned.1.call-update) | async-done | bytes 2359312 | tf_op jit(solution)/shard_map/all_gather | solution.py:195
  179.8 33.9 %while.31 = (s32[]{:T(128)}, bf16[3,512,3,64]{1,3,2,0:T(8,128)(2,1)}, f32[3,3,512]{2,1,0:T(4,128)S(1)}, s32[3]{0:T(128)S(1)}, s32[1536]{0:T(1024)S(1)}, /*index=...) while((s32[]{:T(128)}, ...), condition=%wide.region_6.7_spmd, body=%wide.region_3.6_spmd.sunk | while | flops 633076224 | bytes 38029568 | solution.py:92
  232.6 156.8 %all-reduce.11.cloned.1.call-done = f32[1536,768]{0,1:T(8,128)} async-done(((f32[1536,768]{0,1:T(8,128)}), f32[1536,768]{0,1:T(8,128)}) %all-reduce.11.cloned.1.call-update) | async-done | bytes 4718608 | tf_op jit(solution)/shard_map/psum | solution.py:210
  421.9 171.2 %all-reduce.13.cloned.1.call-done = f32[1536,768]{0,1:T(8,128)} async-done(((f32[1536,768]{0,1:T(8,128)}), f32[1536,768]{0,1:T(8,128)}) %all-reduce.13.cloned.1.call-update) | async-done | bytes 4718608 | tf_op jit(solution)/shard_map/psum | solution.py:218
  601.2 9.5 all_gather.34
  633.7 169.7 %all-reduce.15.cloned.1.call-done = f32[1536,768]{0,1:T(8,128)} async-done(((f32[1536,768]{0,1:T(8,128)}), f32[1536,768]{0,1:T(8,128)}) %all-reduce.15.cloned.1.call-update) | async-done | bytes 4718608 | tf_op jit(solution)/shard_map/psum | solution.py:258
  821.4 161.7 %while.32 = (s32[]{:T(128)}, f32[1,1536,3,64]{1,3,2,0:T(8,128)}, f32[1,1536,3,64]{1,3,2,0:T(8,128)S(1)}, f32[3,512,3,64]{1,0,3,2:T(4,128)}, s32[3]{0:T(128)S(1)}...) while((s32[]{:T(128)}, f32[1,1536,3,64]{1,3,2,0:T(8,128)}, ...), condition=%wide.region_29.30_spmd.clone, body=%wide.region_26.29_spmd.clone.sunk | while | flops 1534130688 | bytes 86367704 | solution.py:137
  839.3 9.4 multiply_convert_fusion.4
  893.0 9.4 multiply_convert_fusion.4
  993.0 171.1 %all-reduce.17.cloned.1.call-done = f32[1536,768]{0,1:T(8,128)} async-done(((f32[1536,768]{0,1:T(8,128)}), f32[1536,768]{0,1:T(8,128)}) %all-reduce.17.cloned.1.call-update) | async-done | bytes 4718608 | tf_op jit(solution)/shard_map/psum | solution.py:283
  1166.3 21.2 %scatter_custom_fusion = f32[30528,192]{1,0:T(8,128)} fusion(s32[1536]{0:T(1024)} %copy-done.49, f32[1536,192]{1,0:T(8,128)S(1)} %copy.157, f32[]{:T(128)} %constant.228.clone.1), kind=kCustom, calls=%fused_computation.51 | custom fusion | flops 294912 | bytes 23446016 | tf_op jit(solution)/shard_map/scatter-add | solution.py:288
  1201.7 15.3 fusion.50
  1224.7 151.4 %reduce-scatter.11.cloned.1.call-done = f32[3816,192]{1,0:T(8,128)} async-done(((f32[30528,192]{1,0:T(8,128)}), f32[3816,192]{1,0:T(8,128)}) %reduce-scatter.11.cloned.1.call-update) | async-done | bytes 2930704 | tf_op jit(solution)/shard_map/reduce_scatter | solution.py:292
  1381.2 12.6 copy.160
  1393.8 28.0 %reduce-scatter.17.cloned.1.call-done = f32[768,96]{0,1:T(8,128)} async-done(((f32[768,768]{0,1:T(8,128)}), f32[768,96]{0,1:T(8,128)}) %reduce-scatter.17.cloned.1.call-update) | async-done | bytes 294928 | tf_op jit(solution)/shard_map/reduce_scatter | solution.py:296
  1423.5 36.1 %reduce-scatter.21.cloned.1.call-done = f32[96,2]{1,0:T(8,128)} async-done(((f32[768,2]{1,0:T(8,128)}), f32[96,2]{1,0:T(8,128)}) %reduce-scatter.21.cloned.1.call-update) | async-done | bytes 784
  1461.8 36.2 %reduce-scatter.19.cloned.1.call-done = f32[96,192]{1,0:T(8,128)} async-done(((f32[768,192]{1,0:T(8,128)}), f32[96,192]{1,0:T(8,128)}) %reduce-scatter.19.cloned.1.call-update) | async-done | bytes 73744
  1499.6 56.7 %reduce-scatter.15.cloned.1.call-done = f32[96,2,768]{2,0,1:T(8,128)} async-done(((f32[768,2,768]{2,0,1:T(8,128)}), f32[96,2,768]{2,0,1:T(8,128)}) %reduce-scatter.15.cloned.1.call-update) | async-done | bytes 589840 | tf_op jit(solution)/shard_map/reduce_scatter | solution.py:295
  1558.1 44.5 %reduce-scatter.13.cloned.1.call-done = f32[96,3,192]{2,0,1:T(8,128)} async-done(((f32[768,3,192]{2,0,1:T(8,128)}), f32[96,3,192]{2,0,1:T(8,128)}) %reduce-scatter.13.cloned.1.call-update) | async-done | bytes 221200 | tf_op jit(solution)/shard_map/reduce_scatter | solution.py:293
  1611.3 13.3 copy.158
  1624.7 53.5 %psum.39 = f32[]{:T(128)} all-reduce(f32[]{:T(128)S(6)} %add.324), channel_id=1, replica_groups=mesh['batch'=8,'mp'=4] {'batch','mp'}, use_global_device_ids=true, to_apply=%region_46.47 | all-reduce | flops 1 | bytes 8 | tf_op jit(solution)/shard_map/psum | solution.py:303
  1687.7 123.4 %all-gather.13.cloned.1.call-done = f32[3816,768]{0,1:T(8,128)} async-done(((f32[3816,192]{0,1:T(8,128)}), f32[3816,768]{0,1:T(8,128)}) %all-gather.13.cloned.1.call-update) | async-done | bytes 11722768 | tf_op jit(solution)/shard_map/all_gather | solution.py:302
  1811.0 17.3 fusion.46
  1828.4 12.3 copy.169
  1840.7 22.2 %fusion.45 = f32[3816,768]{0,1:T(8,128)} fusion(f32[3816,768]{0,1:T(8,128)} %copy.141, f32[3816,768]{0,1:T(8,128)} %get-tuple-element.440, f32[3816,768]{0,1:T(8,128)} %copy.158, f32[3816,768]{0,1:T(8,128)} %copy.160), kind=kLoop, calls=%fused_computation.57 | loop fusion | flops 41029632 | bytes 58613760 | tf_op jit(solution)/shard_map/sub | solution.py:147
  1862.9 12.3 copy.167
  1875.3 12.4 copy.171
  (347 shorter events, 350.5 us)
Async XLA Ops:
  7.2 87.3 %all-gather.17.cloned.1.call-start = ((), (), s32[]{:S(2)}) async-start(), calls=%async_computation.18 | async-start | bytes 13271040 | tf_op jit(solution)/shard_map/all_gather | solution.py:181
  22.8 152.7 %all-gather.15.cloned.1.call-start = ((), (), s32[]{:S(2)}) async-start(), calls=%async_computation.17 | async-start | bytes 2949120 | tf_op jit(solution)/shard_map/all_gather | solution.py:195
  31.4 81.2 %copy-start.49 = (s32[1536]{0:T(1024)}, s32[1536]{0:T(1024)S(1)}, u32[]{:S(2)}) copy-start(s32[1536]{0:T(1024)S(1)} %fusion.104) | copy-start | bytes 18436
  124.8 103.5 %all-gather.9.cloned.1.call-start = ((), (), s32[]{:S(2)}) async-start(), calls=%async_computation.7 | async-start | bytes 2654208 | tf_op jit(solution)/shard_map/all_gather | solution.py:184
  125.7 263.7 %all-reduce.11.cloned.1.call-start = ((), (), s32[]{:S(2)}) async-start(), calls=%async_computation.6 | async-start | bytes 9437184 | tf_op jit(solution)/shard_map/psum | solution.py:210
  151.1 64.4 %copy-start.10 = (bf16[192,768]{0,1:T(8,128)(2,1)}, bf16[192,768]{0,1:T(8,128)(2,1)S(1)}, u32[]{:S(2)}) copy-start(bf16[192,768]{0,1:T(8,128)(2,1)S(1)} %all_gather.30) | copy-start | bytes 884740
  218.5 196.3 %all-gather.11.cloned.1.call-start = ((), (), s32[]{:S(2)}) async-start(), calls=%async_computation.8 | async-start | bytes 1327104 | tf_op jit(solution)/shard_map/all_gather | solution.py:185
  219.2 373.9 %all-reduce.13.cloned.1.call-start = ((), (), s32[]{:S(2)}) async-start(), calls=%async_computation.9 | async-start | bytes 9437184 | tf_op jit(solution)/shard_map/psum | solution.py:218
  228.3 585.8 %copy-start.45 = (f32[768]{0:T(1024)}, f32[768]{0:T(1024)S(1)}, u32[]{:S(2)}) copy-start(f32[768]{0:T(1024)S(1)} %get-tuple-element.396) | copy-start | bytes 9220
  393.4 420.7 %copy-start.41 = (f32[1536]{0:T(1024)}, f32[1536]{0:T(1024)S(1)}, u32[]{:S(2)}) copy-start(f32[1536]{0:T(1024)S(1)} %broadcast_multiply_fusion.3) | copy-start | bytes 18436
  393.9 420.1 %copy-start.43 = (f32[1536]{0:T(1024)}, f32[1536]{0:T(1024)S(1)}, u32[]{:S(2)}) copy-start(f32[1536]{0:T(1024)S(1)} %fusion.101) | copy-start | bytes 18436
  421.0 382.4 %all-reduce.15.cloned.1.call-start = ((), (), s32[]{:S(2)}) async-start(), calls=%async_computation.10 | async-start | bytes 9437184 | tf_op jit(solution)/shard_map/psum | solution.py:258
  617.5 185.9 %copy-start.47 = (f32[1536]{0:T(1024)}, f32[1536]{0:T(1024)S(1)}, u32[]{:S(2)}) copy-start(f32[1536]{0:T(1024)S(1)} %negate_multiply_fusion.1) | copy-start | bytes 18436
  633.2 530.8 %all-reduce.17.cloned.1.call-start = ((), (), s32[]{:S(2)}) async-start(), calls=%async_computation.11 | async-start | bytes 9437184 | tf_op jit(solution)/shard_map/psum | solution.py:283
  821.4 163.9 %copy-start.20 = (f32[1536,32]{0,1:T(8,128)S(1)}, f32[1536,32]{0,1:T(8,128)}, u32[]{:S(2)}) copy-start(f32[1536,32]{0,1:T(8,128)} %copy-done.19) | copy-start | bytes 589828
  992.9 383.2 %reduce-scatter.11.cloned.1.call-start = ((), (), s32[]{:S(2)}) async-start(), calls=%async_computation.12 | async-start | bytes 35168256 | tf_op jit(solution)/shard_map/reduce_scatter | solution.py:292
  1187.5 234.4 %reduce-scatter.17.cloned.1.call-start = ((), (), s32[]{:S(2)}) async-start(), calls=%async_computation.15 | async-start | bytes 2654208 | tf_op jit(solution)/shard_map/reduce_scatter | solution.py:296
  1194.9 264.7 %reduce-scatter.21.cloned.1.call-start = ((), (), s32[]{:S(2)}) async-start(), calls=%async_computation.20 | async-start | bytes 442368
  1196.0 302.0 %reduce-scatter.19.cloned.1.call-start = ((), (), s32[]{:S(2)}) async-start(), calls=%async_computation.19 | async-start | bytes 884736
  1201.7 354.7 %reduce-scatter.15.cloned.1.call-start = ((), (), s32[]{:S(2)}) async-start(), calls=%async_computation.14 | async-start | bytes 5308416 | tf_op jit(solution)/shard_map/reduce_scatter | solution.py:295
  1217.1 385.6 %reduce-scatter.13.cloned.1.call-start = ((), (), s32[]{:S(2)}) async-start(), calls=%async_computation.13 | async-start | bytes 2654208 | tf_op jit(solution)/shard_map/reduce_scatter | solution.py:293
  1224.7 586.4 %all-gather.13.cloned.1.call-start = ((), (), s32[]{:S(2)}) async-start(), calls=%async_computation.16 | async-start | bytes 14745600 | tf_op jit(solution)/shard_map/all_gather | solution.py:302
  1611.3 67.6 %copy-start.13 = (f32[96,2,768]{2,1,0:T(2,128)S(1)}, f32[96,2,768]{2,1,0:T(2,128)}, u32[]{:S(2)}) copy-start(f32[96,2,768]{2,1,0:T(2,128)} %param.37) | copy-start | bytes 1769476
  1611.3 67.6 %copy-start.14 = (f32[96,2,768]{2,0,1:T(8,128)S(1)}, f32[96,2,768]{2,0,1:T(8,128)}, u32[]{:S(2)}) copy-start(f32[96,2,768]{2,0,1:T(8,128)} %reduce-scatter.15.cloned.1.call-done) | copy-start | bytes 1769476
  1611.3 67.6 %copy-start.31 = (f32[96,2,768]{2,1,0:T(2,128)S(1)}, f32[96,2,768]{2,1,0:T(2,128)}, u32[]{:S(2)}) copy-start(f32[96,2,768]{2,1,0:T(2,128)} %param.43) | copy-start | bytes 1769476
  1611.3 67.6 %copy-start.32 = (f32[96,2,768]{2,1,0:T(2,128)S(1)}, f32[96,2,768]{2,1,0:T(2,128)}, u32[]{:S(2)}) copy-start(f32[96,2,768]{2,1,0:T(2,128)} %param.49) | copy-start | bytes 1769476
  1624.6 58.6 %copy-start.55 = (f32[2,96]{1,0:T(2,128)S(1)}, f32[2,96]{1,0:T(2,128)}, u32[]{:S(2)}) copy-start(f32[2,96]{1,0:T(2,128)} %param.45) | copy-start | bytes 2308
  1624.6 58.6 %copy-start.56 = (f32[2,96]{1,0:T(2,128)S(1)}, f32[2,96]{1,0:T(2,128)}, u32[]{:S(2)}) copy-start(f32[2,96]{1,0:T(2,128)} %param.51) | copy-start | bytes 2308
  1624.6 59.2 %copy-start.36 = (f32[192,96]{1,0:T(8,128)S(1)}, f32[192,96]{1,0:T(8,128)}, u32[]{:S(2)}) copy-start(f32[192,96]{1,0:T(8,128)} %param.36) | copy-start | bytes 221188
  1624.6 60.9 %copy-start.24 = (f32[768,96]{0,1:T(8,128)S(1)}, f32[768,96]{0,1:T(8,128)}, u32[]{:S(2)}) copy-start(f32[768,96]{0,1:T(8,128)} %param.38) | copy-start | bytes 884740
  1624.6 60.9 %copy-start.27 = (f32[768,96]{0,1:T(8,128)S(1)}, f32[768,96]{0,1:T(8,128)}, u32[]{:S(2)}) copy-start(f32[768,96]{0,1:T(8,128)} %reduce-scatter.17.cloned.1.call-done) | copy-start | bytes 884740
  1624.6 60.9 %copy-start.37 = (f32[768,96]{0,1:T(8,128)S(1)}, f32[768,96]{0,1:T(8,128)}, u32[]{:S(2)}) copy-start(f32[768,96]{0,1:T(8,128)} %param.44) | copy-start | bytes 884740
  (53 other events, 413.0 us)
Sparse Core Ops, SparseCore 0:
  22.9 71.4 all-gather.16
  125.0 50.4 all-gather.14
  178.0 27.8 all-gather.8
  218.6 170.7 all-reduce.10
  391.7 23.0 all-gather.10
  421.1 171.9 all-reduce.12
  633.3 170.0 all-reduce.14
  993.0 170.9 all-reduce.16
  1187.6 188.4 reduce-scatter.10
  1379.3 42.5 reduce-scatter.16
  1425.8 33.7 reduce-scatter.20
  1463.0 34.9 reduce-scatter.18
  1502.4 53.8 reduce-scatter.14
  1560.1 42.5 reduce-scatter.12
  1604.7 206.2 all-gather.12
where the time goes:
time: 1900 us
  waiting for transfers between devices  1240 us (65%)
  local copies, waits for them, and re-layouts  191 us (10%)
  matrix products  179 us (9%)
  other arithmetic  153 us (8%)
  blocking collectives  94.2 us (5%)
  between operations  21.7 us (1%)
    psum x1, waiting for transfers between devices, local(): lax.psum(jnp.dot(active_low, w_down, preferred_element_type=jnp.float32),...  171 us
    psum x1, waiting for transfers between devices, local(): lax.psum(contract(grad_qkv_low, w_qkv.reshape(D, -1), 1, 1), 'mp')  171 us
    psum x1, waiting for transfers between devices, local(): grad_one = grad_second + lax.psum(back_term, 'mp')  170 us
    psum x1, waiting for transfers between devices, local(): attn = lax.psum(attn_term, 'mp')  157 us
    reduce_scatter x1, waiting for transfers between devices, local(): lax.psum_scatter(grad_table, 'batch', scatter_dimension=0, tiled=True)  151 us
    all_gather x1, waiting for transfers between devices, local(): table_full = lax.all_gather(reduced[0], 'mp', axis=1, tiled=True)  123 us
    unnamed x132, local copies, waits for them, and re-layouts  102 us
    unnamed x17, waiting for transfers between devices  72.6 us
  transfers between devices with their start and end apart: 15, of which 14 were waited for; matrix products, arithmetic and copies ran while one was open for 8% of the time, Pallas kernels for 0%

commit v1 on v0

--- a/solution.py
+++ b/solution.py
@@ -13,6 +13,34 @@
 step_number = 3.0
 rates = (0.3, 0.02, 0.02, 0.02, 0.02, 0.3)
 negative = -1e30
+
+
+def load_gates_by_axis(here_x, axis_k):
+    here_x = jnp.moveaxis(here_x, 0, axis_k)
+    piece_next = here_x.shape
+    return here_x.reshape(
+        *piece_next[:axis_k], piece_next[axis_k] * piece_next[axis_k + 1], *piece_next[axis_k + 2 :]
+    )
+
+
+def loops_extend(q_in, chip_axis):
+    local_out = lax.axis_size(chip_axis)
+    reply = lax.axis_index(chip_axis)
+    ready, work_now = (local_out, reply)
+    mixed_arr, known = (q_in[None], 1)
+    while known < ready:
+        row_list = []
+        rr = 0
+        while rr < ready:
+            row_list.append((rr, rr ^ known))
+            rr += 1
+        z2 = lax.ppermute(mixed_arr, axis_name=chip_axis, perm=row_list)
+        e_next = work_now & known == 0
+        arr_next = jnp.where(e_next, mixed_arr, z2)
+        v_now = jnp.where(e_next, z2, mixed_arr)
+        mixed_arr = jnp.concatenate([arr_next, v_now])
+        known *= 2
+    return mixed_arr
 
 
 def positions(segment_row, segment_count):
@@ -177,8 +205,13 @@
     local_width = table.shape[1] // lax.axis_size("mp")
     column = lax.axis_index("mp") * local_width
     table_cols = lax.dynamic_slice_in_dim(table, column, local_width, 1)
+
+    def match_results(block_here, x_part, along_dim):
+        block_next = loops_extend(block_here, x_part)
+        return load_gates_by_axis(block_next, along_dim)
+
     low_table, w_qkv, w_out, w_gu, w_down, gain_low = (
-        lax.all_gather(table_cols.astype(jnp.bfloat16), "batch", axis=0, tiled=True),
+        match_results(table_cols.astype(jnp.bfloat16), "batch", 0),
         lax.all_gather(qkv_weight.astype(jnp.bfloat16), "batch", axis=0, tiled=True),
         lax.all_gather(out_weight.astype(jnp.bfloat16), "batch", axis=1, tiled=True),
         lax.all_gather(gate_up_weight.astype(jnp.bfloat16), "batch", axis=0, tiled=True),

time: 1900 us -> 2050 us (1.079)
  waiting for transfers between devices: 1240 us -> 1360 us
    ppermute x0 -> x3, waiting for transfers between devices: none -> 186 us  [loops_extend(): z2 = lax.ppermute(mixed_arr, axis_name=chip_axis, perm=row_list)]
    all_gather x1 -> x0, waiting for transfers between devices: 63.1 us -> none  [local(): lax.all_gather(table_cols.astype(jnp.bfloat16), 'batch', axis=0, tiled=True)]
    unnamed x132 -> x137, local copies, waits for them, and re-layouts: 102 us -> 101 us
    unnamed x17 -> x16, waiting for transfers between devices: 72.6 us -> 72.5 us
  transfers between devices with their start and end apart: 15 -> 17, of which waited for: 14 -> 16; matrix products, arithmetic and copies ran while one was open for 8% -> 7% of each run, Pallas kernels for 0% -> 0%
where the time goes in v1:
time: 2050 us; the launch traced here: 2040 us
  waiting for transfers between devices  1360 us (66%)
  local copies, waits for them, and re-layouts  191 us (9%)
  matrix products  179 us (9%)
  other arithmetic  172 us (8%)
  blocking collectives  93.9 us (5%)
  between operations  21.7 us (1%)
    ppermute x3, waiting for transfers between devices, loops_extend(): z2 = lax.ppermute(mixed_arr, axis_name=chip_axis, perm=row_list)  186 us
    psum x1, waiting for transfers between devices, local(): lax.psum(jnp.dot(active_low, w_down, preferred_element_type=jnp.float32),...  171 us
    psum x1, waiting for transfers between devices, local(): lax.psum(contract(grad_qkv_low, w_qkv.reshape(D, -1), 1, 1), 'mp')  171 us
    psum x1, waiting for transfers between devices, local(): grad_one = grad_second + lax.psum(back_term, 'mp')  170 us
    psum x1, waiting for transfers between devices, local(): attn = lax.psum(attn_term, 'mp')  157 us
    reduce_scatter x1, waiting for transfers between devices, local(): lax.psum_scatter(grad_table, 'batch', scatter_dimension=0, tiled=True)  151 us
    all_gather x1, waiting for transfers between devices, local(): table_full = lax.all_gather(reduced[0], 'mp', axis=1, tiled=True)  123 us
    unnamed x137, local copies, waits for them, and re-layouts  101 us
  transfers between devices with their start and end apart: 17, of which 16 were waited for; matrix products, arithmetic and copies ran while one was open for 7% of the time, Pallas kernels for 0%

profile of v1, /device:TPU:0, one launch (start us, length us, event | category | flops | bytes accessed | tf_op | source)
XLA Modules:
  0.0 2043.4 jit_solution(2420443045732905145)
XLA Ops:
  7.3 12.4 copy.141
  31.8 64.3 %collective-permute-done.1 = bf16[2,3816,192]{1,2,0:T(8,128)(2,1)} collective-permute-done((bf16[2,3816,192]{1,2,0:T(8,128)(2,1)S(1)}, bf16[2,3816,192]{1,2,0:T(8,128)(2,1)}, u32[]{:S(2)}, u32[]{:S(2)}) %collective-permute-start.1) | collective-permute-done | bytes 2930720 | tf_op jit(solution)/shard_map/ppermute | solution.py:37
  112.8 118.7 %collective-permute-done.2 = bf16[4,3816,192]{1,2,0:T(8,128)(2,1)} collective-permute-done((bf16[4,3816,192]{1,2,0:T(8,128)(2,1)}, bf16[4,3816,192]{1,2,0:T(8,128)(2,1)}, u32[]{:S(2)}, u32[]{:S(2)}) %collective-permute-start.2) | collective-permute-done | bytes 5861408 | tf_op jit(solution)/shard_map/ppermute | solution.py:37
  241.0 18.1 copy.142
  259.1 11.2 gather_fusion.1
  272.5 13.1 all_gather.25
  298.1 25.1 %all-gather.13.cloned.1.call-done = bf16[1536,768]{0,1:T(8,128)(2,1)} async-done(((bf16[1536,192]{0,1:T(8,128)(2,1)}), bf16[1536,768]{0,1:T(8,128)(2,1)}) %all-gather.13.cloned.1.call-update) | async-done | bytes 2359312 | tf_op jit(solution)/shard_map/all_gather | solution.py:228
  327.5 33.9 %while.31 = (s32[]{:T(128)}, bf16[3,512,3,64]{1,3,2,0:T(8,128)(2,1)}, f32[3,3,512]{2,1,0:T(4,128)S(1)}, s32[3]{0:T(128)S(1)}, s32[1536]{0:T(1024)S(1)}, /*index=...) while((s32[]{:T(128)}, ...), condition=%wide.region_6.7_spmd, body=%wide.region_3.6_spmd.sunk | while | flops 633076224 | bytes 38029568 | solution.py:120
  380.3 156.8 %all-reduce.11.cloned.1.call-done = f32[1536,768]{0,1:T(8,128)} async-done(((f32[1536,768]{0,1:T(8,128)}), f32[1536,768]{0,1:T(8,128)}) %all-reduce.11.cloned.1.call-update) | async-done | bytes 4718608 | tf_op jit(solution)/shard_map/psum | solution.py:243
  569.6 171.3 %all-reduce.13.cloned.1.call-done = f32[1536,768]{0,1:T(8,128)} async-done(((f32[1536,768]{0,1:T(8,128)}), f32[1536,768]{0,1:T(8,128)}) %all-reduce.13.cloned.1.call-update) | async-done | bytes 4718608 | tf_op jit(solution)/shard_map/psum | solution.py:251
  749.0 9.5 all_gather.30
  781.4 169.7 %all-reduce.15.cloned.1.call-done = f32[1536,768]{0,1:T(8,128)} async-done(((f32[1536,768]{0,1:T(8,128)}), f32[1536,768]{0,1:T(8,128)}) %all-reduce.15.cloned.1.call-update) | async-done | bytes 4718608 | tf_op jit(solution)/shard_map/psum | solution.py:291
  969.1 161.7 %while.32 = (s32[]{:T(128)}, f32[1,1536,3,64]{1,3,2,0:T(8,128)}, f32[1,1536,3,64]{1,3,2,0:T(8,128)S(1)}, f32[3,512,3,64]{1,0,3,2:T(4,128)}, s32[3]{0:T(128)S(1)}...) while((s32[]{:T(128)}, f32[1,1536,3,64]{1,3,2,0:T(8,128)}, ...), condition=%wide.region_29.30_spmd.clone, body=%wide.region_26.29_spmd.clone.sunk | while | flops 1534130688 | bytes 86367704 | solution.py:165
  987.0 9.4 multiply_convert_fusion.4
  1140.7 171.1 %all-reduce.17.cloned.1.call-done = f32[1536,768]{0,1:T(8,128)} async-done(((f32[1536,768]{0,1:T(8,128)}), f32[1536,768]{0,1:T(8,128)}) %all-reduce.17.cloned.1.call-update) | async-done | bytes 4718608 | tf_op jit(solution)/shard_map/psum | solution.py:316
  1314.0 21.2 %scatter_custom_fusion = f32[30528,192]{1,0:T(8,128)} fusion(s32[1536]{0:T(1024)} %copy-done.52, f32[1536,192]{1,0:T(8,128)S(1)} %copy.157, f32[]{:T(128)} %constant.231.clone.1), kind=kCustom, calls=%fused_computation.51 | custom fusion | flops 294912 | bytes 23446016 | tf_op jit(solution)/shard_map/scatter-add | solution.py:321
  1349.4 15.3 fusion.50
  1372.4 151.4 %reduce-scatter.11.cloned.1.call-done = f32[3816,192]{1,0:T(8,128)} async-done(((f32[30528,192]{1,0:T(8,128)}), f32[3816,192]{1,0:T(8,128)}) %reduce-scatter.11.cloned.1.call-update) | async-done | bytes 2930704 | tf_op jit(solution)/shard_map/reduce_scatter | solution.py:325
  1528.9 12.6 copy.160
  1541.5 28.2 %reduce-scatter.17.cloned.1.call-done = f32[768,96]{0,1:T(8,128)} async-done(((f32[768,768]{0,1:T(8,128)}), f32[768,96]{0,1:T(8,128)}) %reduce-scatter.17.cloned.1.call-update) | async-done | bytes 294928 | tf_op jit(solution)/shard_map/reduce_scatter | solution.py:329
  1571.4 36.0 %reduce-scatter.21.cloned.1.call-done = f32[96,2]{1,0:T(8,128)} async-done(((f32[768,2]{1,0:T(8,128)}), f32[96,2]{1,0:T(8,128)}) %reduce-scatter.21.cloned.1.call-update) | async-done | bytes 784
  1609.5 36.4 %reduce-scatter.19.cloned.1.call-done = f32[96,192]{1,0:T(8,128)} async-done(((f32[768,192]{1,0:T(8,128)}), f32[96,192]{1,0:T(8,128)}) %reduce-scatter.19.cloned.1.call-update) | async-done | bytes 73744
  1647.4 56.6 %reduce-scatter.15.cloned.1.call-done = f32[96,2,768]{2,0,1:T(8,128)} async-done(((f32[768,2,768]{2,0,1:T(8,128)}), f32[96,2,768]{2,0,1:T(8,128)}) %reduce-scatter.15.cloned.1.call-update) | async-done | bytes 589840 | tf_op jit(solution)/shard_map/reduce_scatter | solution.py:328
  1705.9 44.6 %reduce-scatter.13.cloned.1.call-done = f32[96,3,192]{2,0,1:T(8,128)} async-done(((f32[768,3,192]{2,0,1:T(8,128)}), f32[96,3,192]{2,0,1:T(8,128)}) %reduce-scatter.13.cloned.1.call-update) | async-done | bytes 221200 | tf_op jit(solution)/shard_map/reduce_scatter | solution.py:326
  1759.1 13.3 copy.158
  1772.5 53.5 %psum.39 = f32[]{:T(128)} all-reduce(f32[]{:T(128)S(6)} %add.324), channel_id=1, replica_groups=mesh['batch'=8,'mp'=4] {'batch','mp'}, use_global_device_ids=true, to_apply=%region_46.47 | all-reduce | flops 1 | bytes 8 | tf_op jit(solution)/shard_map/psum | solution.py:336
  1835.5 123.4 %all-gather.11.cloned.1.call-done = f32[3816,768]{0,1:T(8,128)} async-done(((f32[3816,192]{0,1:T(8,128)}), f32[3816,768]{0,1:T(8,128)}) %all-gather.11.cloned.1.call-update) | async-done | bytes 11722768 | tf_op jit(solution)/shard_map/all_gather | solution.py:335
  1958.9 17.3 fusion.46
  1976.2 12.3 copy.169
  1988.5 22.2 %fusion.45 = f32[3816,768]{0,1:T(8,128)} fusion(f32[3816,768]{0,1:T(8,128)} %copy.141, f32[3816,768]{0,1:T(8,128)} %get-tuple-element.440, f32[3816,768]{0,1:T(8,128)} %copy.158, f32[3816,768]{0,1:T(8,128)} %copy.160), kind=kLoop, calls=%fused_computation.57 | loop fusion | flops 41029632 | bytes 58613760 | tf_op jit(solution)/shard_map/sub | solution.py:175
  2010.8 12.3 copy.167
  2023.1 12.4 copy.171
  (362 shorter events, 386.2 us)
Async XLA Ops:
  7.2 97.2 %copy-start = (s32[30528]{0:T(1024)S(1)}, s32[30528]{0:T(1024)}, u32[]{:S(2)}) copy-start(s32[30528]{0:T(1024)} %param.32) | copy-start | bytes 366340
  7.2 316.0 %all-gather.13.cloned.1.call-start = ((), (), s32[]{:S(2)}) async-start(), calls=%async_computation.17 | async-start | bytes 2949120 | tf_op jit(solution)/shard_map/all_gather | solution.py:228
  21.7 3.4 collective-permute-start
  28.9 67.2 %collective-permute-start.1 = (bf16[2,3816,192]{1,2,0:T(8,128)(2,1)S(1)}, bf16[2,3816,192]{1,2,0:T(8,128)(2,1)}, u32[]{:S(2)}, u32[]{:S(2)}) collective-permute-start(bf16[2,3816,192]{1,2,0:T(8,128)(2,1)S(1)} %pad_maximum_fusion.2), channel_id=1, source_target_pairs={{0,8},{4,12},{8,0},{12,4},{16,24},{20,28},{24,16},{28,20},{1,9},{5... | collective-permute-start | bytes 8792072 | tf_op jit(solution)/shard_map/ppermute | solution.py:37
  102.6 128.9 %collective-permute-start.2 = (bf16[4,3816,192]{1,2,0:T(8,128)(2,1)}, bf16[4,3816,192]{1,2,0:T(8,128)(2,1)}, u32[]{:S(2)}, u32[]{:S(2)}) collective-permute-start(bf16[4,3816,192]{1,2,0:T(8,128)(2,1)} %pad_maximum_fusion.1), channel_id=1, source_target_pairs={{0,16},{4,20},{8,24},{12,28},{16,0},{20,4},{24,8},{28,12},{1,17},{... | collective-permute-start | bytes 17584136 | tf_op jit(solution)/shard_map/ppermute | solution.py:37
  112.8 123.1 %copy-start.52 = (s32[1536]{0:T(1024)}, s32[1536]{0:T(1024)S(1)}, u32[]{:S(2)}) copy-start(s32[1536]{0:T(1024)S(1)} %fusion.104) | copy-start | bytes 18436
  271.4 104.6 %all-gather.7.cloned.1.call-start = ((), (), s32[]{:S(2)}) async-start(), calls=%async_computation.7 | async-start | bytes 2654208 | tf_op jit(solution)/shard_map/all_gather | solution.py:217
  272.2 264.9 %all-reduce.11.cloned.1.call-start = ((), (), s32[]{:S(2)}) async-start(), calls=%async_computation.6 | async-start | bytes 9437184 | tf_op jit(solution)/shard_map/psum | solution.py:243
  297.3 65.8 %copy-start.13 = (bf16[192,768]{0,1:T(8,128)(2,1)}, bf16[192,768]{0,1:T(8,128)(2,1)S(1)}, u32[]{:S(2)}) copy-start(bf16[192,768]{0,1:T(8,128)(2,1)S(1)} %all_gather.26) | copy-start | bytes 884740
  366.2 196.3 %all-gather.9.cloned.1.call-start = ((), (), s32[]{:S(2)}) async-start(), calls=%async_computation.8 | async-start | bytes 1327104 | tf_op jit(solution)/shard_map/all_gather | solution.py:218
  366.9 373.9 %all-reduce.13.cloned.1.call-start = ((), (), s32[]{:S(2)}) async-start(), calls=%async_computation.9 | async-start | bytes 9437184 | tf_op jit(solution)/shard_map/psum | solution.py:251
  376.0 585.8 %copy-start.48 = (f32[768]{0:T(1024)}, f32[768]{0:T(1024)S(1)}, u32[]{:S(2)}) copy-start(f32[768]{0:T(1024)S(1)} %get-tuple-element.396) | copy-start | bytes 9220
  541.1 420.7 %copy-start.44 = (f32[1536]{0:T(1024)}, f32[1536]{0:T(1024)S(1)}, u32[]{:S(2)}) copy-start(f32[1536]{0:T(1024)S(1)} %broadcast_multiply_fusion.3) | copy-start | bytes 18436
  541.6 420.1 %copy-start.46 = (f32[1536]{0:T(1024)}, f32[1536]{0:T(1024)S(1)}, u32[]{:S(2)}) copy-start(f32[1536]{0:T(1024)S(1)} %fusion.101) | copy-start | bytes 18436
  568.7 382.4 %all-reduce.15.cloned.1.call-start = ((), (), s32[]{:S(2)}) async-start(), calls=%async_computation.10 | async-start | bytes 9437184 | tf_op jit(solution)/shard_map/psum | solution.py:291
  765.3 185.8 %copy-start.50 = (f32[1536]{0:T(1024)}, f32[1536]{0:T(1024)S(1)}, u32[]{:S(2)}) copy-start(f32[1536]{0:T(1024)S(1)} %negate_multiply_fusion.1) | copy-start | bytes 18436
  780.9 530.8 %all-reduce.17.cloned.1.call-start = ((), (), s32[]{:S(2)}) async-start(), calls=%async_computation.11 | async-start | bytes 9437184 | tf_op jit(solution)/shard_map/psum | solution.py:316
  969.1 163.9 %copy-start.23 = (f32[1536,32]{0,1:T(8,128)S(1)}, f32[1536,32]{0,1:T(8,128)}, u32[]{:S(2)}) copy-start(f32[1536,32]{0,1:T(8,128)} %copy-done.22) | copy-start | bytes 589828
  1140.6 383.2 %reduce-scatter.11.cloned.1.call-start = ((), (), s32[]{:S(2)}) async-start(), calls=%async_computation.12 | async-start | bytes 35168256 | tf_op jit(solution)/shard_map/reduce_scatter | solution.py:325
  1335.2 234.5 %reduce-scatter.17.cloned.1.call-start = ((), (), s32[]{:S(2)}) async-start(), calls=%async_computation.15 | async-start | bytes 2654208 | tf_op jit(solution)/shard_map/reduce_scatter | solution.py:329
  1342.6 264.7 %reduce-scatter.21.cloned.1.call-start = ((), (), s32[]{:S(2)}) async-start(), calls=%async_computation.19 | async-start | bytes 442368
  1343.7 302.1 %reduce-scatter.19.cloned.1.call-start = ((), (), s32[]{:S(2)}) async-start(), calls=%async_computation.18 | async-start | bytes 884736
  1349.4 354.7 %reduce-scatter.15.cloned.1.call-start = ((), (), s32[]{:S(2)}) async-start(), calls=%async_computation.14 | async-start | bytes 5308416 | tf_op jit(solution)/shard_map/reduce_scatter | solution.py:328
  1364.8 385.7 %reduce-scatter.13.cloned.1.call-start = ((), (), s32[]{:S(2)}) async-start(), calls=%async_computation.13 | async-start | bytes 2654208 | tf_op jit(solution)/shard_map/reduce_scatter | solution.py:326
  1372.4 586.5 %all-gather.11.cloned.1.call-start = ((), (), s32[]{:S(2)}) async-start(), calls=%async_computation.16 | async-start | bytes 14745600 | tf_op jit(solution)/shard_map/all_gather | solution.py:335
  1759.1 67.6 %copy-start.16 = (f32[96,2,768]{2,1,0:T(2,128)S(1)}, f32[96,2,768]{2,1,0:T(2,128)}, u32[]{:S(2)}) copy-start(f32[96,2,768]{2,1,0:T(2,128)} %param.37) | copy-start | bytes 1769476
  1759.1 67.6 %copy-start.17 = (f32[96,2,768]{2,0,1:T(8,128)S(1)}, f32[96,2,768]{2,0,1:T(8,128)}, u32[]{:S(2)}) copy-start(f32[96,2,768]{2,0,1:T(8,128)} %reduce-scatter.15.cloned.1.call-done) | copy-start | bytes 1769476
  1759.1 67.6 %copy-start.34 = (f32[96,2,768]{2,1,0:T(2,128)S(1)}, f32[96,2,768]{2,1,0:T(2,128)}, u32[]{:S(2)}) copy-start(f32[96,2,768]{2,1,0:T(2,128)} %param.43) | copy-start | bytes 1769476
  1759.1 67.6 %copy-start.35 = (f32[96,2,768]{2,1,0:T(2,128)S(1)}, f32[96,2,768]{2,1,0:T(2,128)}, u32[]{:S(2)}) copy-start(f32[96,2,768]{2,1,0:T(2,128)} %param.49) | copy-start | bytes 1769476
  1772.4 60.9 %copy-start.27 = (f32[768,96]{0,1:T(8,128)S(1)}, f32[768,96]{0,1:T(8,128)}, u32[]{:S(2)}) copy-start(f32[768,96]{0,1:T(8,128)} %param.38) | copy-start | bytes 884740
  1772.4 60.9 %copy-start.30 = (f32[768,96]{0,1:T(8,128)S(1)}, f32[768,96]{0,1:T(8,128)}, u32[]{:S(2)}) copy-start(f32[768,96]{0,1:T(8,128)} %reduce-scatter.17.cloned.1.call-done) | copy-start | bytes 884740
  1772.5 60.9 %copy-start.40 = (f32[768,96]{0,1:T(8,128)S(1)}, f32[768,96]{0,1:T(8,128)}, u32[]{:S(2)}) copy-start(f32[768,96]{0,1:T(8,128)} %param.44) | copy-start | bytes 884740
  (58 other events, 575.9 us)
Sparse Core Ops, SparseCore 0:
  271.5 51.6 all-gather.12
  325.7 27.8 all-gather.6
  366.3 170.7 all-reduce.10
  539.4 23.0 all-gather.8
  568.8 171.9 all-reduce.12
  781.0 170.0 all-reduce.14
  1140.7 170.9 all-reduce.16
  1335.3 188.4 reduce-scatter.10
  1527.2 42.5 reduce-scatter.16
  1573.5 33.7 reduce-scatter.20
  1610.8 34.9 reduce-scatter.18
  1650.1 53.8 reduce-scatter.14
  1707.9 42.4 reduce-scatter.12
  1752.5 206.2 all-gather.10
